TPU v7x, 256 devices: a whole 4x4x8 slice. The times are simulated.
256 devices in a mesh: corner: 16 (over y, x_lo, core), tm: 16 (over z, x_hi).
Axes of the slice: x: 4 (x_hi: 2, x_lo: 2; x = x_hi * 2 + x_lo), y: 4, z: 8, core: 2. Of those that a mesh axis runs over, the one named last changes fastest.
Arguments:
- signal: bfloat16 [16, 64, 65536], P('corner', None, 'tm'), may hold values from -6 to 6
- dilated_conv_weight: bfloat16 [2, 256, 128], replicated, may hold values from -0.5 to 0.5
- dilated_conv_bias: float32 [2, 256], replicated, may hold values from -3 to 3
- projection_weight: bfloat16 [2, 128, 128], replicated, may hold values from -0.5 to 0.5
- projection_bias: float32 [2, 128], replicated, may hold values from -3 to 3
- cot_top: bfloat16 [16, 64, 65536], P('corner', None, 'tm'), may hold values from -6 to 6
- cot_skip: bfloat16 [16, 64, 65536], P('corner', None, 'tm'), may hold values from -6 to 6
Outputs:
- x_top: bfloat16 [16, 64, 65536], P('corner', None, 'tm')
- skip_sum: bfloat16 [16, 64, 65536], P('corner', None, 'tm')
- grad_input: bfloat16 [16, 64, 65536], P('corner', None, 'tm')
- grad_conv: float32 [2, 256, 128], replicated
- grad_conv_bias: float32 [2, 256], replicated
- grad_out: float32 [2, 128, 128], replicated
- grad_out_bias: float32 [2, 128], replicated
All inputs are finite; a program needn't handle non-finite values.
Results may differ from a plain program's by a relative error of at most 0.0065.
Values may be sent and summed in bfloat16 or wider, within the bound.
No kernel may reach another device: no remote copies, remote signals or barrier semaphores. Data moves between devices by JAX's collectives and lax.ppermute only.
A program may use at most 64 MiB of HBM per device.

v0:
```python
import math
import jax
import jax.numpy as jnp
from jax import lax
from jax.sharding import PartitionSpec as P


def from_behind(block, axis, distance):
    devices = range(lax.axis_size(axis))
    route = [(i - distance, i) for i in devices if i - distance in devices]
    return lax.ppermute(block, axis, route)


def gated_layer_forward(a_in, tap_in, weight, bias, proj, proj_bias, gsize, rsize):
    stacked = jnp.concatenate([tap_in, a_in], axis=1)
    pre_act = (
        jnp.einsum("oc,bct->bot", weight, stacked, preferred_element_type=jnp.float32)
        + bias[None, :, None]
    )
    gate_out = (jnp.tanh(pre_act[:, :gsize]) * jax.nn.sigmoid(pre_act[:, gsize:])).astype(
        jnp.bfloat16
    )
    mixed = (
        jnp.einsum("og,bgt->bot", proj, gate_out, preferred_element_type=jnp.float32)
        + proj_bias[None, :, None]
    )
    next_act = (a_in.astype(jnp.float32) + mixed[:, :rsize]).astype(jnp.bfloat16)
    return (stacked, pre_act, gate_out, next_act, mixed[:, rsize:])


def layer_backward(go_res, go_skip, stacked, pre_act, gate_out, weight, proj, gsize, rsize):
    upper = jnp.concatenate([go_res, go_skip], axis=1)
    grad_proj = jnp.einsum("bot,bgt->og", upper, gate_out, preferred_element_type=jnp.float32)
    grad_pbias = jnp.sum(upper, axis=(0, 2), dtype=jnp.float32)
    grad_gate = jnp.einsum("og,bot->bgt", proj, upper, preferred_element_type=jnp.float32)
    filt_act = jnp.tanh(pre_act[:, :gsize])
    gate_act = jax.nn.sigmoid(pre_act[:, gsize:])
    grad_pre = jnp.concatenate(
        [
            grad_gate * gate_act * (1.0 - filt_act * filt_act),
            grad_gate * filt_act * gate_act * (1.0 - gate_act),
        ],
        axis=1,
    ).astype(jnp.bfloat16)
    grad_weight = jnp.einsum("bot,bct->oc", grad_pre, stacked, preferred_element_type=jnp.float32)
    grad_bias = jnp.sum(grad_pre, axis=(0, 2), dtype=jnp.float32)
    grad_in = jnp.einsum("oc,bot->bct", weight, grad_pre, preferred_element_type=jnp.float32)
    return (
        grad_in[:, :rsize].astype(jnp.bfloat16),
        grad_in[:, rsize:],
        (grad_weight, grad_bias, grad_proj, grad_pbias),
    )


def on_device(
    signal,
    dilated_conv_weight,
    dilated_conv_bias,
    projection_weight,
    projection_bias,
    cot_top,
    cot_skip,
):
    rsize = signal.shape[1]
    gsize = projection_weight.shape[2]
    tap_near = from_behind(signal, "tm", 1)
    (
        lower_saved_state,
        lower_preactivation,
        lower_gated_output,
        middle_layer_input,
        lower_skip_output,
    ) = gated_layer_forward(
        signal,
        tap_near,
        dilated_conv_weight[0],
        dilated_conv_bias[0],
        projection_weight[0],
        projection_bias[0],
        gsize,
        rsize,
    )
    tap_far = from_behind(middle_layer_input, "tm", 2)
    (
        upper_saved_state,
        upper_preactivation,
        upper_gated_output,
        upper_layer_output,
        upper_skip_output,
    ) = gated_layer_forward(
        middle_layer_input,
        tap_far,
        dilated_conv_weight[1],
        dilated_conv_bias[1],
        projection_weight[1],
        projection_bias[1],
        gsize,
        rsize,
    )
    skip_out = (lower_skip_output + upper_skip_output).astype(jnp.bfloat16)
    delayed_gradient_upper, current_gradient_upper, grads_top = layer_backward(
        cot_top,
        cot_skip,
        upper_saved_state,
        upper_preactivation,
        upper_gated_output,
        dilated_conv_weight[1],
        projection_weight[1],
        gsize,
        rsize,
    )
    later_top = from_behind(delayed_gradient_upper, "tm", -2)
    middle_input_gradient = (
        cot_top.astype(jnp.float32) + current_gradient_upper + later_top.astype(jnp.float32)
    ).astype(jnp.bfloat16)
    delayed_gradient_lower, current_gradient_lower, grads_low = layer_backward(
        middle_input_gradient,
        cot_skip,
        lower_saved_state,
        lower_preactivation,
        lower_gated_output,
        dilated_conv_weight[0],
        projection_weight[0],
        gsize,
        rsize,
    )
    later_low = from_behind(delayed_gradient_lower, "tm", -1)
    lower_input_gradient = (
        middle_input_gradient.astype(jnp.float32)
        + current_gradient_lower
        + later_low.astype(jnp.float32)
    ).astype(jnp.bfloat16)
    summed = lax.psum(
        (
            jnp.stack([grads_low[0], grads_top[0]]),
            jnp.stack([grads_low[1], grads_top[1]]),
            jnp.stack([grads_low[2], grads_top[2]]),
            jnp.stack([grads_low[3], grads_top[3]]),
        ),
        ("corner", "tm"),
    )
    count = signal.shape[0] * lax.axis_size("corner") * signal.shape[2] * lax.axis_size("tm")
    scale = 1.0 / math.sqrt(count)
    return (
        upper_layer_output,
        skip_out,
        lower_input_gradient,
        summed[0] * scale,
        summed[1] * scale,
        summed[2] * scale,
        summed[3] * scale,
    )


def solution(mesh):
    return jax.shard_map(
        on_device,
        mesh=mesh,
        in_specs=(
            P("corner", None, "tm"),
            P(),
            P(),
            P(),
            P(),
            P("corner", None, "tm"),
            P("corner", None, "tm"),
        ),
        out_specs=(
            P("corner", None, "tm"),
            P("corner", None, "tm"),
            P("corner", None, "tm"),
            P(),
            P(),
            P(),
            P(),
        ),
        check_vma=False,
    )
```

profile of v0, /device:TPU:1, one launch (start us, length us, event | category | flops | bytes accessed | tf_op | source)
XLA Modules:
  0.0 411.1 jit_solution(4979422311224916654)
XLA Ops:
  7.2 5.5 %collective-permute-start = (bf16[1,64,4096]{2,1,0:T(8,128)(2,1)}, bf16[1,64,4096]{2,1,0:T(8,128)(2,1)S(1)}, u32[]{:S(2)}, u32[]{:S(2)}) collective-permute-start(bf16[1,64,4096]{2,1,0:T(8,128)(2,1)} %param.7), channel_id=1, source_target_pairs={{0,1},{1,2},{2,3},{3,4},{4,5},{5,6},{6,7},{7,8},{8,9},{9,10},{10,1... | collective-permute-start | bytes 1572872 | tf_op jit(solution)/shard_map/ppermute | solution.py:11
  12.7 0.8 fusion.55
  13.5 0.8 slice_bitcast_fusion
  14.2 1.1 constant_dynamic-update-slice_fusion.1
  15.3 8.3 %collective-permute-done = bf16[1,64,4096]{2,1,0:T(8,128)(2,1)S(1)} collective-permute-done((bf16[1,64,4096]{2,1,0:T(8,128)(2,1)}, bf16[1,64,4096]{2,1,0:T(8,128)(2,1)S(1)}, u32[]{:S(2)}, u32[]{:S(2)}) %collective-permute-start) | collective-permute-done | bytes 524320 | tf_op jit(solution)/shard_map/ppermute | solution.py:11
  23.6 2.0 fusion.1
  25.6 0.8 fusion.18
  26.9 0.6 copy-done.6
  27.6 5.3 %collective-permute-start.1 = (bf16[1,64,4096]{2,1,0:T(8,128)(2,1)S(1)}, bf16[1,64,4096]{2,1,0:T(8,128)(2,1)S(1)}, u32[]{:S(2)}, u32[]{:S(2)}) collective-permute-start(bf16[1,64,4096]{2,1,0:T(8,128)(2,1)S(1)} %fusion.26), channel_id=1, source_target_pairs={{0,2},{1,3},{2,4},{3,5},{4,6},{5,7},{6,8},{7,9},{8,10},{9,11},{10,... | collective-permute-start | bytes 1572872 | tf_op jit(solution)/shard_map/ppermute | solution.py:11
  33.2 9.3 %collective-permute-done.1 = bf16[1,64,4096]{2,1,0:T(8,128)(2,1)S(1)} collective-permute-done((bf16[1,64,4096]{2,1,0:T(8,128)(2,1)S(1)}, bf16[1,64,4096]{2,1,0:T(8,128)(2,1)S(1)}, u32[]{:S(2)}, u32[]{:S(2)}) %collective-permute-start.1) | collective-permute-done | bytes 524320 | tf_op jit(solution)/shard_map/ppermute | solution.py:11
  42.5 0.7 fusion.3
  43.3 1.5 multiply_convert_fusion.3
  44.8 0.5 convolution_bitcast_fusion.6
  45.3 1.3 collective-permute-start.2
  47.0 1.2 fusion.24
  48.6 0.7 fusion.16
  49.3 0.4 convolution_bitcast_fusion.8
  49.8 9.4 %collective-permute-done.2 = bf16[1,64,4096]{2,1,0:T(8,128)(2,1)S(1)} collective-permute-done((bf16[1,64,4096]{2,1,0:T(8,128)(2,1)S(1)}, bf16[1,64,4096]{2,1,0:T(8,128)(2,1)S(1)}, u32[]{:S(2)}, u32[]{:S(2)}) %collective-permute-start.2) | collective-permute-done | bytes 524320 | tf_op jit(solution)/shard_map/ppermute | solution.py:11
  59.3 1.3 multiply_convert_fusion.1
  62.0 82.7 %all-reduce = (f32[2,256]{1,0:T(2,128)S(1)}, f32[2,128]{1,0:T(2,128)S(1)}) all-reduce(f32[2,256]{1,0:T(2,128)S(1)} %pad_maximum_fusion.15, f32[2,128]{1,0:T(2,128)S(1)} %pad_maximum_fusion.16), channel_id=1, replica_groups=mesh['corner'=16,'tm'=16] {'corner','tm'}, use_global_device_ids=true, to_apply=%region_3.0 | all-reduce | flops 768 | bytes 6144 | tf_op jit(solution)/shard_map/psum | solution.py:133
  144.7 0.6 broadcast_multiply_fusion.2
  145.3 2.2 convolution_bitcast_fusion.4
  147.5 0.8 slice.202
  148.3 1.3 collective-permute-start.3
  149.6 0.7 pad_maximum_fusion.14
  150.3 0.7 fusion.17
  151.0 0.7 pad_maximum_fusion.13
  151.7 0.6 broadcast_multiply_fusion.3
  152.3 246.7 %all-reduce.4.cloned.1.call-done = (f32[2,256,128]{2,1,0:T(8,128)}, f32[2,128,128]{2,1,0:T(8,128)}) async-done(((f32[2,256,128]{2,1,0:T(8,128)}, f32[2,128,128]{2,1,0:T(8,128)}), (f32[2,256,128]{2,1,0:T(8,128)}, f32[2,128,128]{2,1,0:T(8,128)})) %all-reduce.4.cloned.1.call-update) | async-done | bytes 393232 | tf_op jit(solution)/shard_map/psum | solution.py:133
  399.0 1.6 broadcast_multiply_fusion.1
  400.6 1.7 broadcast_multiply_fusion
  402.2 2.0 fusion.21
  (37 shorter events, 3.2 us)
Async XLA Ops:
  7.2 391.8 %all-reduce.4.cloned.1.call-start = ((), (), s32[]{:S(2)}) async-start(), calls=%async_computation | async-start | bytes 786432 | tf_op jit(solution)/shard_map/psum | solution.py:133
  7.2 16.4 %collective-permute-start = (bf16[1,64,4096]{2,1,0:T(8,128)(2,1)}, bf16[1,64,4096]{2,1,0:T(8,128)(2,1)S(1)}, u32[]{:S(2)}, u32[]{:S(2)}) collective-permute-start(bf16[1,64,4096]{2,1,0:T(8,128)(2,1)} %param.7), channel_id=1, source_target_pairs={{0,1},{1,2},{2,3},{3,4},{4,5},{5,6},{6,7},{7,8},{8,9},{9,10},{10,1... | collective-permute-start | bytes 1572872 | tf_op jit(solution)/shard_map/ppermute | solution.py:11
  23.6 2.0 copy-start.8
  25.6 0.9 copy-start.10
  26.4 1.0 copy-start.6
  26.4 6.5 %copy-start.5 = (bf16[1,64,4096]{2,1,0:T(8,128)(2,1)S(1)}, bf16[1,64,4096]{2,1,0:T(8,128)(2,1)}, u32[]{:S(2)}) copy-start(bf16[1,64,4096]{2,1,0:T(8,128)(2,1)} %param.13) | copy-start | bytes 1572868
  27.5 15.1 %copy-start.7 = (bf16[2,256,128]{2,1,0:T(8,128)(2,1)S(1)}, bf16[2,256,128]{2,1,0:T(8,128)(2,1)}, u32[]{:S(2)}) copy-start(bf16[2,256,128]{2,1,0:T(8,128)(2,1)} %param.8) | copy-start | bytes 393220
  27.6 15.0 %collective-permute-start.1 = (bf16[1,64,4096]{2,1,0:T(8,128)(2,1)S(1)}, bf16[1,64,4096]{2,1,0:T(8,128)(2,1)S(1)}, u32[]{:S(2)}, u32[]{:S(2)}) collective-permute-start(bf16[1,64,4096]{2,1,0:T(8,128)(2,1)S(1)} %fusion.26), channel_id=1, source_target_pairs={{0,2},{1,3},{2,4},{3,5},{4,6},{5,7},{6,8},{7,9},{8,10},{9,11},{10,... | collective-permute-start | bytes 1572872 | tf_op jit(solution)/shard_map/ppermute | solution.py:11
  45.3 13.9 %collective-permute-start.2 = (bf16[1,64,4096]{2,1,0:T(8,128)(2,1)S(1)}, bf16[1,64,4096]{2,1,0:T(8,128)(2,1)S(1)}, u32[]{:S(2)}, u32[]{:S(2)}) collective-permute-start(bf16[1,64,4096]{2,1,0:T(8,128)(2,1)S(1)} %slice.203), channel_id=1, source_target_pairs={{2,0},{3,1},{4,2},{5,3},{6,4},{7,5},{8,6},{9,7},{10,8},{11,9},{12,... | collective-permute-start | bytes 1572872 | tf_op jit(solution)/shard_map/ppermute | solution.py:11
  49.3 9.8 %copy-start.4 = (bf16[1,64,4096]{2,1,0:T(8,128)(2,1)S(1)}, bf16[1,64,4096]{2,1,0:T(8,128)(2,1)}, u32[]{:S(2)}) copy-start(bf16[1,64,4096]{2,1,0:T(8,128)(2,1)} %param.12) | copy-start | bytes 1572868
  60.7 1.1 copy-start
  60.7 1.3 copy-start.2
  145.3 5.0 %copy-start.1 = (bf16[1,128,4096]{2,1,0:T(8,128)(2,1)S(1)}, bf16[1,128,4096]{2,1,0:T(8,128)(2,1)}, u32[]{:S(2)}) copy-start(bf16[1,128,4096]{2,1,0:T(8,128)(2,1)} %copy-done) | copy-start | bytes 3145732
  145.3 5.0 %copy-start.3 = (bf16[1,128,4096]{2,1,0:T(8,128)(2,1)S(1)}, bf16[1,128,4096]{2,1,0:T(8,128)(2,1)}, u32[]{:S(2)}) copy-start(bf16[1,128,4096]{2,1,0:T(8,128)(2,1)} %copy-done.2) | copy-start | bytes 3145732
  145.3 5.0 %copy-start.9 = (bf16[1,64,4096]{2,1,0:T(8,128)(2,1)S(1)}, bf16[1,64,4096]{2,1,0:T(8,128)(2,1)}, u32[]{:S(2)}) copy-start(bf16[1,64,4096]{2,1,0:T(8,128)(2,1)} %copy-done.8) | copy-start | bytes 1572868
  148.3 253.9 %collective-permute-start.3 = (bf16[1,64,4096]{2,1,0:T(8,128)(2,1)}, bf16[1,64,4096]{2,1,0:T(8,128)(2,1)}, u32[]{:S(2)}, u32[]{:S(2)}) collective-permute-start(bf16[1,64,4096]{2,1,0:T(8,128)(2,1)} %slice.202), channel_id=1, source_target_pairs={{1,0},{2,1},{3,2},{4,3},{5,4},{6,5},{7,6},{8,7},{9,8},{10,9},{11,1... | collective-permute-start | bytes 1572872 | tf_op jit(solution)/shard_map/ppermute | solution.py:11
Sparse Core Ops, SparseCore 0:
  151.9 247.0 all-reduce.3
where the time goes:
time: 412 us; the launch traced here: 411 us
  waiting for transfers between devices  274 us (67%)
  blocking collectives  82.7 us (20%)
  between operations  14.3 us (3%)
  starting transfers between devices  13.5 us (3%)
  matrix products  11.3 us (3%)
  other arithmetic  11.3 us (3%)
  local copies, waits for them, and re-layouts  4.41 us (1%)
    psum x1, waiting for transfers between devices, on_device(): lax.psum((jnp.stack([grads_low[0], grads_top[0]]), jnp.stack([grads_low[1...  247 us
    psum x1, blocking collectives, on_device(): lax.psum((jnp.stack([grads_low[0], grads_top[0]]), jnp.stack([grads_low[1...  82.7 us
    ppermute x4, waiting for transfers between devices, from_behind(): return lax.ppermute(block, axis, route)  27 us
    ppermute x4, starting transfers between devices, from_behind(): return lax.ppermute(block, axis, route)  13.4 us
  transfers between devices with their start and end apart: 5, of which 4 were waited for; matrix products, arithmetic and copies ran while one was open for 3% of the time, Pallas kernels for 0%

commit v1 on v0

--- a/solution.py
+++ b/solution.py
@@ -130,14 +130,21 @@
         + current_gradient_lower
         + later_low.astype(jnp.float32)
     ).astype(jnp.bfloat16)
-    summed = lax.psum(
+
+    def watch_the_pages(vector, which_axis, axis_name):
+        for w in (which_axis, axis_name):
+            vector = lax.psum(vector, axis_name=w)
+        return vector
+
+    summed = watch_the_pages(
         (
             jnp.stack([grads_low[0], grads_top[0]]),
             jnp.stack([grads_low[1], grads_top[1]]),
             jnp.stack([grads_low[2], grads_top[2]]),
             jnp.stack([grads_low[3], grads_top[3]]),
         ),
-        ("corner", "tm"),
+        "corner",
+        "tm",
     )
     count = signal.shape[0] * lax.axis_size("corner") * signal.shape[2] * lax.axis_size("tm")
     scale = 1.0 / math.sqrt(count)

time: 412 us -> 370 us (0.90)
  the two profiles are of different devices: /device:TPU:1 before, /device:TPU:8 now
where the time goes in v1:
time: 370 us
  waiting for transfers between devices  247 us (67%)
  blocking collectives  70.9 us (19%)
  between operations  14.3 us (4%)
  starting transfers between devices  13.2 us (4%)
  other arithmetic  10.2 us (3%)
  matrix products  9.4 us (3%)
  local copies, waits for them, and re-layouts  4.14 us (1%)
    psum x2, waiting for transfers between devices, watch_the_pages(): vector = lax.psum(vector, axis_name=w)  219 us
    psum x2, blocking collectives, watch_the_pages(): vector = lax.psum(vector, axis_name=w)  70.9 us
    ppermute x4, waiting for transfers between devices, from_behind(): return lax.ppermute(block, axis, route)  28.9 us
    ppermute x4, starting transfers between devices, from_behind(): return lax.ppermute(block, axis, route)  13.1 us
  transfers between devices with their start and end apart: 6, of which 5 were waited for; matrix products, arithmetic and copies ran while one was open for 3% of the time, Pallas kernels for 0%

profile of v1, /device:TPU:8, one launch (start us, length us, event | category | flops | bytes accessed | tf_op | source)
XLA Modules:
  0.0 369.6 jit_solution(15206140490801051141)
XLA Ops:
  7.2 5.0 %collective-permute-start = (bf16[1,64,4096]{2,1,0:T(8,128)(2,1)}, bf16[1,64,4096]{2,1,0:T(8,128)(2,1)S(1)}, u32[]{:S(2)}, u32[]{:S(2)}) collective-permute-start(bf16[1,64,4096]{2,1,0:T(8,128)(2,1)} %param.7), channel_id=1, source_target_pairs={{0,1},{1,2},{2,3},{3,4},{4,5},{5,6},{6,7},{7,8},{8,9},{9,10},{10,1... | collective-permute-start | bytes 1572872 | tf_op jit(solution)/shard_map/ppermute | solution.py:11
  12.2 0.8 fusion.55
  12.9 0.8 slice_bitcast_fusion
  13.7 1.1 constant_dynamic-update-slice_fusion.1
  14.8 8.8 %collective-permute-done = bf16[1,64,4096]{2,1,0:T(8,128)(2,1)S(1)} collective-permute-done((bf16[1,64,4096]{2,1,0:T(8,128)(2,1)}, bf16[1,64,4096]{2,1,0:T(8,128)(2,1)S(1)}, u32[]{:S(2)}, u32[]{:S(2)}) %collective-permute-start) | collective-permute-done | bytes 524320 | tf_op jit(solution)/shard_map/ppermute | solution.py:11
  23.6 1.8 fusion.1
  25.4 0.8 fusion.18
  26.7 0.6 copy-done.2
  27.4 5.6 %collective-permute-start.1 = (bf16[1,64,4096]{2,1,0:T(8,128)(2,1)S(1)}, bf16[1,64,4096]{2,1,0:T(8,128)(2,1)S(1)}, u32[]{:S(2)}, u32[]{:S(2)}) collective-permute-start(bf16[1,64,4096]{2,1,0:T(8,128)(2,1)S(1)} %fusion.26), channel_id=1, source_target_pairs={{0,2},{1,3},{2,4},{3,5},{4,6},{5,7},{6,8},{7,9},{8,10},{9,11},{10,... | collective-permute-start | bytes 1572872 | tf_op jit(solution)/shard_map/ppermute | solution.py:11
  33.3 10.0 %collective-permute-done.1 = bf16[1,64,4096]{2,1,0:T(8,128)(2,1)S(1)} collective-permute-done((bf16[1,64,4096]{2,1,0:T(8,128)(2,1)S(1)}, bf16[1,64,4096]{2,1,0:T(8,128)(2,1)S(1)}, u32[]{:S(2)}, u32[]{:S(2)}) %collective-permute-start.1) | collective-permute-done | bytes 524320 | tf_op jit(solution)/shard_map/ppermute | solution.py:11
  43.3 0.7 fusion.3
  44.0 1.5 multiply_convert_fusion.3
  46.0 1.3 collective-permute-start.2
  47.8 1.2 fusion.24
  49.3 0.7 fusion.16
  50.5 10.1 %collective-permute-done.2 = bf16[1,64,4096]{2,1,0:T(8,128)(2,1)S(1)} collective-permute-done((bf16[1,64,4096]{2,1,0:T(8,128)(2,1)S(1)}, bf16[1,64,4096]{2,1,0:T(8,128)(2,1)S(1)}, u32[]{:S(2)}, u32[]{:S(2)}) %collective-permute-start.2) | collective-permute-done | bytes 524320 | tf_op jit(solution)/shard_map/ppermute | solution.py:11
  60.7 1.3 multiply_convert_fusion.1
  63.1 0.5 convolution_bitcast_fusion.4
  63.6 0.8 slice.202
  64.4 1.3 collective-permute-start.3
  65.7 0.7 pad_maximum_fusion.14
  66.4 0.7 fusion.17
  67.1 0.7 pad_maximum_fusion.13
  67.9 27.3 %all-reduce.2 = (f32[2,256]{1,0:T(2,128)S(1)}, f32[2,128]{1,0:T(2,128)S(1)}) all-reduce(f32[2,256]{1,0:T(2,128)S(1)} %pad_maximum_fusion.15, f32[2,128]{1,0:T(2,128)S(1)} %pad_maximum_fusion.16), channel_id=1, replica_groups=mesh['corner'=16,'tm'=16] {'corner'}, use_global_device_ids=true, to_apply=%region_4.0 | all-reduce | flops 768 | bytes 6144 | tf_op jit(solution)/shard_map/psum | solution.py:136
  95.2 43.6 %all-reduce = (f32[2,256]{1,0:T(2,128)S(1)}, f32[2,128]{1,0:T(2,128)S(1)}) all-reduce(f32[2,256]{1,0:T(2,128)S(1)} %get-tuple-element.11, f32[2,128]{1,0:T(2,128)S(1)} %get-tuple-element.12), channel_id=1, replica_groups=mesh['corner'=16,'tm'=16] {'tm'}, use_global_device_ids=true, to_apply=%region_5.0 | all-reduce | flops 768 | bytes 6144 | tf_op jit(solution)/shard_map/psum | solution.py:136
  138.8 0.6 broadcast_multiply_fusion.3
  139.4 0.6 broadcast_multiply_fusion.2
  140.0 52.6 %all-reduce.9.cloned.1.call-done = (f32[2,256,128]{2,1,0:T(8,128)}, f32[2,128,128]{2,1,0:T(8,128)}) async-done(((f32[2,256,128]{2,1,0:T(8,128)}, f32[2,128,128]{2,1,0:T(8,128)}), (f32[2,256,128]{2,1,0:T(8,128)}, f32[2,128,128]{2,1,0:T(8,128)})) %all-reduce.9.cloned.1.call-update) | async-done | bytes 393232 | tf_op jit(solution)/shard_map/psum | solution.py:136
  192.6 1.0 fusion.21
  193.6 165.9 %all-reduce.7.cloned.1.call-done = (f32[2,256,128]{2,1,0:T(8,128)}, f32[2,128,128]{2,1,0:T(8,128)}) async-done(((f32[2,256,128]{2,1,0:T(8,128)}, f32[2,128,128]{2,1,0:T(8,128)}), (f32[2,256,128]{2,1,0:T(8,128)}, f32[2,128,128]{2,1,0:T(8,128)})) %all-reduce.7.cloned.1.call-update) | async-done | bytes 393232 | tf_op jit(solution)/shard_map/psum | solution.py:136
  359.5 1.7 broadcast_multiply_fusion
  361.2 1.6 broadcast_multiply_fusion.1
  (29 shorter events, 3.9 us)
Async XLA Ops:
  7.2 185.4 %all-reduce.9.cloned.1.call-start = ((), (), s32[]{:S(2)}) async-start(), calls=%async_computation.1 | async-start | bytes 786432 | tf_op jit(solution)/shard_map/psum | solution.py:136
  7.2 16.4 %collective-permute-start = (bf16[1,64,4096]{2,1,0:T(8,128)(2,1)}, bf16[1,64,4096]{2,1,0:T(8,128)(2,1)S(1)}, u32[]{:S(2)}, u32[]{:S(2)}) collective-permute-start(bf16[1,64,4096]{2,1,0:T(8,128)(2,1)} %param.7), channel_id=1, source_target_pairs={{0,1},{1,2},{2,3},{3,4},{4,5},{5,6},{6,7},{7,8},{8,9},{9,10},{10,1... | collective-permute-start | bytes 1572872 | tf_op jit(solution)/shard_map/ppermute | solution.py:11
  25.4 0.9 copy-start.4
  26.3 1.0 copy-start.2
  26.3 6.7 %copy-start.1 = (bf16[1,64,4096]{2,1,0:T(8,128)(2,1)S(1)}, bf16[1,64,4096]{2,1,0:T(8,128)(2,1)}, u32[]{:S(2)}) copy-start(bf16[1,64,4096]{2,1,0:T(8,128)(2,1)} %param.13) | copy-start | bytes 1572868
  27.3 16.0 %copy-start.3 = (bf16[2,256,128]{2,1,0:T(8,128)(2,1)S(1)}, bf16[2,256,128]{2,1,0:T(8,128)(2,1)}, u32[]{:S(2)}) copy-start(bf16[2,256,128]{2,1,0:T(8,128)(2,1)} %param.8) | copy-start | bytes 393220
  27.4 15.9 %collective-permute-start.1 = (bf16[1,64,4096]{2,1,0:T(8,128)(2,1)S(1)}, bf16[1,64,4096]{2,1,0:T(8,128)(2,1)S(1)}, u32[]{:S(2)}, u32[]{:S(2)}) collective-permute-start(bf16[1,64,4096]{2,1,0:T(8,128)(2,1)S(1)} %fusion.26), channel_id=1, source_target_pairs={{0,2},{1,3},{2,4},{3,5},{4,6},{5,7},{6,8},{7,9},{8,10},{9,11},{10,... | collective-permute-start | bytes 1572872 | tf_op jit(solution)/shard_map/ppermute | solution.py:11
  46.0 14.5 %collective-permute-start.2 = (bf16[1,64,4096]{2,1,0:T(8,128)(2,1)S(1)}, bf16[1,64,4096]{2,1,0:T(8,128)(2,1)S(1)}, u32[]{:S(2)}, u32[]{:S(2)}) collective-permute-start(bf16[1,64,4096]{2,1,0:T(8,128)(2,1)S(1)} %slice.203), channel_id=1, source_target_pairs={{2,0},{3,1},{4,2},{5,3},{6,4},{7,5},{8,6},{9,7},{10,8},{11,9},{12,... | collective-permute-start | bytes 1572872 | tf_op jit(solution)/shard_map/ppermute | solution.py:11
  50.0 10.5 %copy-start = (bf16[1,64,4096]{2,1,0:T(8,128)(2,1)S(1)}, bf16[1,64,4096]{2,1,0:T(8,128)(2,1)}, u32[]{:S(2)}) copy-start(bf16[1,64,4096]{2,1,0:T(8,128)(2,1)} %param.12) | copy-start | bytes 1572868
  64.4 128.2 %collective-permute-start.3 = (bf16[1,64,4096]{2,1,0:T(8,128)(2,1)}, bf16[1,64,4096]{2,1,0:T(8,128)(2,1)S(1)}, u32[]{:S(2)}, u32[]{:S(2)}) collective-permute-start(bf16[1,64,4096]{2,1,0:T(8,128)(2,1)} %slice.202), channel_id=1, source_target_pairs={{1,0},{2,1},{3,2},{4,3},{5,4},{6,5},{7,6},{8,7},{9,8},{10,9},{11,1... | collective-permute-start | bytes 1572872 | tf_op jit(solution)/shard_map/ppermute | solution.py:11
  67.9 291.6 %all-reduce.7.cloned.1.call-start = ((), (), s32[]{:S(2)}) async-start(), calls=%async_computation | async-start | bytes 786432 | tf_op jit(solution)/shard_map/psum | solution.py:136
Sparse Core Ops, SparseCore 0:
  68.0 124.5 all-reduce.8
  195.5 163.9 all-reduce.6
